TPU v7x, 128 devices: a whole 4x4x4 slice. The times are simulated.
128 devices in a mesh: src: 8 (over y, x_lo), vox: 16 (over x_hi, z, core).
Axes of the slice: x: 4 (x_hi: 2, x_lo: 2; x = x_hi * 2 + x_lo), y: 4, z: 4, core: 2. Of those that a mesh axis runs over, the one named last changes fastest.
Arguments:
- kappa: float32 [128, 64, 256], P('vox'), may hold values from 0.3 to 3
- mua: float32 [128, 64, 256], P('vox'), may hold values from 0.1 to 2
- prior_forward_fields: float32 [16, 128, 64, 256], P('src', 'vox'), may hold values from -10 to 10
- prior_adjoint_fields: float32 [16, 128, 64, 256], P('src', 'vox'), may hold values from -10 to 10
- source_position: int32 [16], replicated, may hold values from 0 to 2097151
- detector_voxel: int32 [2048], P('vox'), may hold values from 0 to 2097151, as said below
- measured_source: int32 [131072], P(('src', 'vox')), may hold values from 0 to 15, as said below
- measured_detector: int32 [131072], P(('src', 'vox')), may hold values from 0 to 2047, as said below
- measured_data: float32 [131072], P(('src', 'vox')), may hold values from -6 to 6
- measured_weight: float32 [131072], P(('src', 'vox')), may hold values from 0.25 to 4
Outputs:
- grad_mua: float32 [128, 64, 256], P('vox', 'src')
- grad_kappa: float32 [128, 64, 256], P('vox', 'src')
Inputs may be any that keep to these rules, and one draw needn't show every extreme that they name: `measured_source`: in each aligned block of 1024 rows (the rows of one device), at most 512 rows name a source of one group, a group being the 2 sources s with the same s // 2. `measured_detector`: row r names a detector of detector block (r // 1024) % 16, that is one from that block times 128 up to the next block's first. `detector_voxel`: detector d lies in the voxel planes x from (d // 128) * 8 to that plus 8 - 1.
All inputs are finite; a program needn't handle non-finite values.
Results may differ from a plain program's by a relative error of at most 0.0003.
Values sent between devices are 32-bit elements; how exact they have to be, the bound alone decides.
A program may use at most 256 MiB of HBM per device.

v0:
```python
import functools

import jax
import jax.numpy as jnp
from jax import lax
from jax.experimental import pallas as pl
from jax.experimental.pallas import tpu as pltpu
from jax.sharding import PartitionSpec as P

SWEEPS = 6
LOW = SWEEPS
HIGH = SWEEPS + 1
source_gain = 10.0

MESH = pl.DeviceIdType.MESH
F32 = jnp.float32
BF16 = jnp.bfloat16
HI = lax.Precision.HIGHEST
NT = (((1,), (1,)), ((), ()))


def slots(ref, *lead):
    return jnp.stack([ref[(*lead, pl.ds(j, 8, stride=8), slice(None))] for j in range(8)])


def y_next(value, zero_edge):
    wrapped = pltpu.roll(value[:1], 7, 1)
    if zero_edge:
        rows = lax.broadcasted_iota(jnp.int32, wrapped.shape, 1)
        wrapped = jnp.where(rows == 7, 0.0, wrapped)
    return jnp.concatenate([value[1:], wrapped], axis=0)


def y_prev(value, zero_edge):
    wrapped = pltpu.roll(value[-1:], 1, 1)
    if zero_edge:
        rows = lax.broadcasted_iota(jnp.int32, wrapped.shape, 1)
        wrapped = jnp.where(rows == 0, 0.0, wrapped)
    return jnp.concatenate([wrapped, value[:-1]], axis=0)


def z_next(halves, zero_edge):
    lane = lax.broadcasted_iota(jnp.int32, halves[0].shape, halves[0].ndim - 1)
    turned = [pltpu.roll(half, 127, half.ndim - 1) for half in halves]
    last = jnp.where(lane == 127, 0.0, turned[1]) if zero_edge else turned[1]
    return [jnp.where(lane == 127, turned[1], turned[0]), last]


def z_prev(halves, zero_edge):
    lane = lax.broadcasted_iota(jnp.int32, halves[0].shape, halves[0].ndim - 1)
    turned = [pltpu.roll(half, 1, half.ndim - 1) for half in halves]
    first = jnp.where(lane == 0, 0.0, turned[0]) if zero_edge else turned[0]
    return [first, jnp.where(lane == 0, turned[0], turned[1])]


def three_parts(value):
    high = value.astype(BF16)
    rest = value - high.astype(F32)
    middle = rest.astype(BF16)
    low = (rest - middle.astype(F32)).astype(BF16)
    return high.astype(F32), middle.astype(F32), low.astype(F32)


def kernel(
    groups,
    slabs,
    kappa,
    mua,
    prior_fwd,
    prior_adj,
    position,
    det_scalar,
    det_row,
    row_source,
    row_detector,
    row_data,
    row_weight,
    out_mua,
    out_kappa,
    kap,
    mu,
    fwd_in,
    adj_in,
    field,
    other,
    adjf,
    coef,
    drive,
    agg,
    agg_in,
    val,
    val_in,
    det_in,
    zhot,
    picked,
    grad,
    grad_in,
    local_sem,
    halo_send,
    halo_recv,
    det_send,
    det_recv,
    agg_send,
    agg_recv,
    val_send,
    val_recv,
    grad_send,
    grad_recv,
):
    src = lax.axis_index("src")
    vox = lax.axis_index("vox")
    core = lax.rem(vox, 2)
    depth = kappa.shape[0]
    total = LOW + depth + HIGH
    detectors = det_row.shape[1]
    has_low = vox > 0
    has_high = vox < slabs - 1
    below = {"vox": jnp.maximum(vox - 1, 0)}
    above = {"vox": jnp.minimum(vox + 1, slabs - 1)}
    peers = [lax.rem(src + step, groups) for step in range(1, groups)]

    barrier = pltpu.get_barrier_semaphore()

    @pl.when(has_high)
    def _():
        pl.semaphore_signal(barrier, inc=1, device_id=above, device_id_type=MESH)

    @pl.when(has_low)
    def _():
        pl.semaphore_signal(barrier, inc=1, device_id=below, device_id_type=MESH)

    for peer in peers:
        pl.semaphore_signal(barrier, inc=1, device_id={"src": peer}, device_id_type=MESH)

    own = []
    for h in range(2):
        lanes = pl.ds(128 * h, 128)
        own.append(
            [
                pltpu.make_async_copy(
                    kappa.at[:, :, lanes], kap.at[pl.ds(LOW, depth), h], local_sem.at[0, h]
                ),
                pltpu.make_async_copy(
                    mua.at[:, :, lanes], mu.at[pl.ds(LOW, depth), h], local_sem.at[1, h]
                ),
                pltpu.make_async_copy(
                    prior_fwd.at[:, :, :, lanes],
                    fwd_in.at[:, pl.ds(LOW, depth), h],
                    local_sem.at[2, h],
                ),
                pltpu.make_async_copy(
                    prior_adj.at[:, :, :, lanes],
                    adj_in.at[:, pl.ds(LOW, depth), h],
                    local_sem.at[3, h],
                ),
            ]
        )
    for which in range(4):
        for h in range(2):
            own[h][which].start()

    pl.semaphore_wait(
        barrier, groups - 1 + jnp.where(has_low, 1, 0) + jnp.where(has_high, 1, 0)
    )

    def halo(array, direction, h):
        lanes = pl.ds(128 * h, 128)
        if direction == 0:
            count = LOW - 1 if array == 1 else LOW
            start, target = depth - count, LOW - count
        else:
            count = HIGH - 1 if array == 1 else HIGH
            start, target = 0, LOW + depth
        if array < 2:
            source = (kappa, mua)[array].at[pl.ds(start, count), :, lanes]
            place = (kap, mu)[array].at[pl.ds(target, count), h]
        else:
            source = (prior_fwd, prior_adj)[array - 2].at[:, pl.ds(start, count), :, lanes]
            place = (fwd_in, adj_in)[array - 2].at[:, pl.ds(target, count), h]
        return pltpu.make_async_remote_copy(
            src_ref=source,
            dst_ref=place,
            send_sem=halo_send.at[array, direction, h],
            recv_sem=halo_recv.at[array, direction, h],
            device_id=above if direction == 0 else below,
            device_id_type=MESH,
        )

    halos = [[[halo(a, d, h) for h in range(2)] for d in range(2)] for a in range(4)]
    det_copy = [
        pltpu.make_async_remote_copy(
            src_ref=det_row,
            dst_ref=det_in.at[d],
            send_sem=det_send.at[d],
            recv_sem=det_recv.at[d],
            device_id=(above, below)[d],
            device_id_type=MESH,
        )
        for d in range(2)
    ]

    sends_to = (has_high, has_low)
    gets_from = (has_low, has_high)
    for d in range(2):

        @pl.when(sends_to[d])
        def _():
            det_copy[d].start()
            for a in range(4):
                for h in range(2):
                    halos[a][d][h].start()

    for d in range(2):

        @pl.when(jnp.logical_not(gets_from[d]))
        def _():
            if d == 0:
                planes = slice(0, LOW)
            else:
                planes = slice(LOW + depth, total)
            kap[planes] = jnp.zeros_like(kap[planes])
            fwd_in[:, planes] = jnp.zeros_like(fwd_in[:, planes])
            adj_in[:, planes] = jnp.zeros_like(adj_in[:, planes])
            det_in[d] = jnp.zeros_like(det_in[d])
            val_in[d] = jnp.zeros_like(val_in[d])

    rows = lax.broadcasted_iota(jnp.int32, (8 * groups, 128), 0)
    kind = rows % 8
    source_of = rows // 8 * 2 + kind % 2
    det_base = vox * detectors
    det_ids = lax.broadcasted_iota(jnp.int32, (detectors, 128), 0) + det_base
    summed = jnp.zeros((8 * groups, detectors), F32)
    for i in range(row_source.shape[0]):
        weight = row_weight[i : i + 1, :]
        weighted = weight * row_data[i : i + 1, :]
        chosen = jnp.where(kind < 2, weight, jnp.where(kind < 4, weighted, 0.0))
        chosen = jnp.where(row_source[i : i + 1, :] == source_of, chosen, 0.0)
        hot = jnp.where(row_detector[i : i + 1, :] == det_ids, 1.0, 0.0)
        summed = summed + lax.dot_general(
            chosen, hot, NT, precision=HI, preferred_element_type=F32
        )
    agg[...] = summed
    agg_copy = []
    for step, peer in enumerate(peers):
        copy = pltpu.make_async_remote_copy(
            src_ref=agg.at[pl.ds(pl.multiple_of(8 * peer, 8), 8)],
            dst_ref=agg_in.at[src],
            send_sem=agg_send.at[step],
            recv_sem=agg_recv.at[step],
            device_id={"src": peer},
            device_id_type=MESH,
        )
        copy.start()
        agg_copy.append(copy)
    agg_in[src] = agg[pl.ds(pl.multiple_of(8 * src, 8), 8), :]

    def coefficients(low, count):
        def body(i, carry):
            p = low + i
            x = vox * depth + p - LOW
            inside = jnp.logical_and(x >= 0, x < slabs * depth)
            centre = [slots(kap, p, h) for h in range(2)]
            zn, zp = z_next(centre, True), z_prev(centre, True)
            row = lax.broadcasted_iota(jnp.int32, (8, 8, 128), 1) * 8 + lax.broadcasted_iota(
                jnp.int32, (8, 8, 128), 0
            )
            lane = lax.broadcasted_iota(jnp.int32, (8, 8, 128), 2)
            for h in range(2):
                mid = centre[h]
                faces = [
                    0.5 * (slots(kap, p + 1, h) + mid),
                    0.5 * (mid + slots(kap, p - 1, h)),
                    0.5 * (y_next(mid, True) + mid),
                    0.5 * (mid + y_prev(mid, True)),
                    0.5 * (zn[h] + mid),
                    0.5 * (mid + zp[h]),
                ]
                diagonal = slots(mu, p, h)
                for face in faces:
                    diagonal = diagonal + face
                inverse = jnp.where(inside, 1.0 / jnp.where(inside, diagonal, 1.0), 0.0)
                faces[2] = jnp.where(row == 63, 0.0, faces[2])
                faces[3] = jnp.where(row == 0, 0.0, faces[3])
                if h == 1:
                    faces[4] = jnp.where(lane == 127, 0.0, faces[4])
                else:
                    faces[5] = jnp.where(lane == 0, 0.0, faces[5])
                for n in range(6):
                    coef[n, p - 1, h] = faces[n] * inverse
                coef[6, p - 1, h] = inverse
                cell = (x * 64 + row) * 256 + 128 * h + lane
                for s in range(2):
                    spot = position[src * 2 + s]
                    drive[p - 1, s, h] = jnp.where(cell == spot, source_gain * inverse, 0.0)
            return carry

        lax.fori_loop(0, count, body, 0)

    def take_in(source, place, low, count):
        def body(i, carry):
            p = low + i
            for s in range(2):
                for h in range(2):
                    place[p, s, h] = slots(source, s, p, h)
            return carry

        lax.fori_loop(0, count, body, 0)

    def sweep(old, new, low, count):
        def body(i, carry):
            p = low + i
            for s in range(2):
                centre = [old[p, s, h] for h in range(2)]
                zn, zp = z_next(centre, False), z_prev(centre, False)
                for h in range(2):
                    mid = centre[h]
                    value = drive[p - 1, s, h] + coef[0, p - 1, h] * old[p + 1, s, h]
                    value = value + coef[1, p - 1, h] * old[p - 1, s, h]
                    value = value + coef[2, p - 1, h] * y_next(mid, False)
                    value = value + coef[3, p - 1, h] * y_prev(mid, False)
                    value = value + coef[4, p - 1, h] * zn[h]
                    value = value + coef[5, p - 1, h] * zp[h]
                    new[p, s, h] = value
            return carry

        lax.fori_loop(0, count, body, 0)

    def pick(even, odd):
        return jnp.where(core == 0, even, odd)

    def early(k):
        return pick(k, k - LOW) + LOW, pick(depth + LOW + 1 - 2 * k, depth + LOW - 2 * k)

    def late(k):
        return pick(k - LOW, depth - k) + LOW, pick(LOW, LOW + 1)

    def solve(fields, part):
        for k in range(1, SWEEPS + 1):
            low, count = part(k)
            sweep(fields[(k - 1) % 2], fields[k % 2], low, count)

    def await_halo(arrays, near):
        for d in range(2):
            on_core = (1 - d) if near else d
            wanted = jnp.logical_and(core == on_core, gets_from[d])

            @pl.when(wanted)
            def _():
                for a in arrays:
                    for h in range(2):
                        halos[a][d][h].wait_recv()

    for which in range(4):
        for h in range(2):
            own[h][which].wait()
    await_halo((0, 1), True)
    near_low = pick(1, 1 - LOW) + LOW
    near_count = pick(depth + LOW - 1, depth + LOW - 2)
    far_low = pick(1 - LOW, depth - 1) + LOW
    far_count = pick(LOW, LOW + 1)
    coefficients(near_low, near_count)
    await_halo((2,), True)
    take_in(fwd_in, field, pick(0, -LOW) + LOW, pick(depth + HIGH, depth + LOW))
    solve((field, other), early)
    await_halo((3,), True)
    take_in(adj_in, adjf, pick(0, -LOW) + LOW, pick(depth + HIGH, depth + LOW))

    identity = jnp.where(
        lax.broadcasted_iota(jnp.int32, (detectors, 128), 0)
        == lax.broadcasted_iota(jnp.int32, (detectors, 128), 1),
        1.0,
        0.0,
    )
    for d in range(2):

        @pl.when(gets_from[d])
        def _():
            det_copy[d].wait_recv()

    for n in range(3):
        where_row = det_in[n] if n < 2 else det_row[...]
        z_row = jnp.broadcast_to((where_row % 256).astype(F32), (8, detectors))
        z_col = lax.dot_general(identity, z_row, NT, precision=HI, preferred_element_type=F32)
        lane = lax.broadcasted_iota(jnp.int32, (detectors, 256), 1).astype(F32)
        zhot[n] = jnp.where(lane == z_col[:, :1], 1.0, 0.0)

    await_halo((0, 1), False)
    coefficients(far_low, far_count)
    await_halo((2,), False)
    take_in(fwd_in, field, pick(-LOW, depth) + LOW, pick(LOW, HIGH))
    solve((field, other), late)

    def gather(d, carry):
        spot = det_scalar[d] - vox * (depth * 64 * 256)
        spot = jnp.clip(spot, 0, depth * 64 * 256 - 1)
        p = spot // (64 * 256)
        y = spot // 256 % 64
        for s in range(2):
            for h in range(2):
                picked[s, h, pl.ds(d, 1), :] = field[p + LOW, s, h, y % 8, pl.ds(y // 8, 1), :]
        return carry

    lax.fori_loop(0, detectors, gather, 0)
    for copy in agg_copy:
        copy.wait()
    sums = agg_in[0]
    for g in range(1, groups):
        sums = sums + agg_in[g]
    predicted = []
    for s in range(2):
        both = picked[s, 0] * zhot[2, :, :128] + picked[s, 1] * zhot[2, :, 128:]
        predicted.append(
            lax.dot_general(
                jnp.ones((8, 128), F32), both, NT, precision=HI, preferred_element_type=F32
            )
        )
    rows8 = lax.broadcasted_iota(jnp.int32, (8, detectors), 0)
    val[...] = sums * jnp.where(rows8 == 0, predicted[0], predicted[1]) - pltpu.roll(sums, 6, 0)
    val_copy = [
        pltpu.make_async_remote_copy(
            src_ref=val,
            dst_ref=val_in.at[d],
            send_sem=val_send.at[d],
            recv_sem=val_recv.at[d],
            device_id=(above, below)[d],
            device_id_type=MESH,
        )
        for d in range(2)
    ]
    for d in range(2):

        @pl.when(sends_to[d])
        def _():
            val_copy[d].start()

    def place_totals(n, totals, where_row, base, low, count):
        spot = where_row - (vox * depth + base) * (64 * 256)
        y = spot // 256 % 64
        code = spot // (64 * 256) * 64 + y % 8 * 8 + y // 8
        parts = [three_parts(totals[s : s + 1]) for s in range(2)]
        hot = zhot[n].astype(BF16)
        hot = jnp.concatenate([hot, hot, hot], axis=0)

        def body(i, carry):
            p = low + i
            rows64 = lax.broadcasted_iota(jnp.int32, (64, detectors), 0) + (p - base) * 64
            match = rows64 == code
            for s in range(2):
                left = [jnp.where(match, part, 0.0).astype(BF16) for part in parts[s]]
                value = lax.dot_general(
                    jnp.concatenate(left, axis=1),
                    hot,
                    (((1,), (0,)), ((), ())),
                    preferred_element_type=F32,
                )
                for h in range(2):
                    half = value[:, 128 * h : 128 * h + 128].reshape(8, 8, 128)
                    drive[p + LOW - 1, s, h] = half * coef[6, p + LOW - 1, h]
            return carry

        lax.fori_loop(0, count, body, 0)

    place_totals(2, val[...], det_row[...], 0, 0, depth)

    def await_values(near):
        for d in range(2):
            on_core = (1 - d) if near else d

            @pl.when(core == on_core)
            def _():
                @pl.when(gets_from[d])
                def _():
                    val_copy[d].wait_recv()

                if d == 0:
                    place_totals(0, val_in[0], det_in[0], -depth, 1 - LOW, LOW - 1)
                else:
                    place_totals(1, val_in[1], det_in[1], depth, depth, HIGH - 1)

    await_values(True)
    solve((adjf, other), early)
    await_values(False)
    await_halo((3,), False)
    take_in(adj_in, adjf, pick(-LOW, depth) + LOW, pick(LOW, HIGH))
    solve((adjf, other), late)

    tile = 64 // groups
    half_depth = depth // 2

    def gradient(i, carry):
        p = i + LOW
        mua_sum = [jnp.zeros((8, 8, 128), F32) for _ in range(2)]
        kap_sum = [jnp.zeros((8, 8, 128), F32) for _ in range(2)]
        for s in range(2):
            f = [field[p, s, h] for h in range(2)]
            a = [adjf[p, s, h] for h in range(2)]
            fz, az = z_next(f, True), z_next(a, True)
            for h in range(2):
                mua_sum[h] = mua_sum[h] - f[h] * a[h]
                product = (field[p + 1, s, h] - f[h]) * (adjf[p + 1, s, h] - a[h])
                product = product + (y_next(f[h], True) - f[h]) * (y_next(a[h], True) - a[h])
                product = product + (fz[h] - f[h]) * (az[h] - a[h])
                kap_sum[h] = kap_sum[h] - product
        for h in range(2):
            for j in range(8):
                grad[0, i, h, pl.ds(j, 8, stride=8), :] = mua_sum[h][j]
                grad[1, i, h, pl.ds(j, 8, stride=8), :] = kap_sum[h][j]
        return carry

    grad_copy = []
    for part in range(2):
        lax.fori_loop(part * half_depth, (part + 1) * half_depth, gradient, 0)
        planes = pl.ds(part * half_depth, half_depth)
        for step, peer in enumerate(peers):
            copy = pltpu.make_async_remote_copy(
                src_ref=grad.at[:, planes, :, pl.ds(pl.multiple_of(tile * peer, 8), tile)],
                dst_ref=grad_in.at[step, :, planes],
                send_sem=grad_send.at[part, step],
                recv_sem=grad_recv.at[part, step],
                device_id={"src": peer},
                device_id_type=MESH,
            )
            copy.start()
            grad_copy.append(copy)

    for d in range(2):

        @pl.when(sends_to[d])
        def _():
            det_copy[d].wait_send()
            val_copy[d].wait_send()
            for a in range(4):
                for h in range(2):
                    halos[a][d][h].wait_send()

    for copy in grad_copy:
        copy.wait()
    mine = pl.ds(pl.multiple_of(tile * src, 8), tile)
    for q, out in ((0, out_mua), (1, out_kappa)):
        for h in range(2):
            value = grad[q, :, h, mine, :]
            for step in range(groups - 1):
                value = value + grad_in[step, q, :, h]
            out[:, :, 128 * h : 128 * h + 128] = value


def body(
    kappa,
    mua,
    prior_forward_fields,
    prior_adjoint_fields,
    source_position,
    detector_voxel,
    measured_source,
    measured_detector,
    measured_data,
    measured_weight,
):
    groups = lax.axis_size("src")
    slabs = lax.axis_size("vox")
    depth, width, _ = kappa.shape
    total = LOW + depth + HIGH
    detectors = detector_voxel.shape[0]
    blocks = (-1, 128)
    hbm = pl.BlockSpec(memory_space=pl.ANY)
    vmem = pl.BlockSpec(memory_space=pltpu.VMEM)
    smem = pl.BlockSpec(memory_space=pltpu.SMEM)
    tile = width // groups
    dma = pltpu.SemaphoreType.DMA
    slab_field = pltpu.VMEM((total, 2, 2, 8, 8, 128), F32)
    return pl.pallas_call(
        functools.partial(kernel, groups, slabs),
        out_shape=(jax.ShapeDtypeStruct((depth, tile, 256), F32),) * 2,
        in_specs=[hbm] * 4 + [smem] * 2 + [vmem] * 5,
        out_specs=(vmem, vmem),
        scratch_shapes=[
            pltpu.VMEM((total, 2, 64, 128), F32),
            pltpu.VMEM((total, 2, 64, 128), F32),
            pltpu.VMEM((2, total, 2, 64, 128), F32),
            pltpu.VMEM((2, total, 2, 64, 128), F32),
            slab_field,
            slab_field,
            slab_field,
            pltpu.VMEM((7, total - 2, 2, 8, 8, 128), F32),
            pltpu.VMEM((total - 2, 2, 2, 8, 8, 128), F32),
            pltpu.VMEM((8 * groups, detectors), F32),
            pltpu.VMEM((groups, 8, detectors), F32),
            pltpu.VMEM((8, detectors), F32),
            pltpu.VMEM((2, 8, detectors), F32),
            pltpu.VMEM((2, 1, detectors), jnp.int32),
            pltpu.VMEM((3, detectors, 256), F32),
            pltpu.VMEM((2, 2, detectors, 128), F32),
            pltpu.VMEM((2, depth, 2, 64, 128), F32),
            pltpu.VMEM((groups - 1, 2, depth, 2, tile, 128), F32),
            dma((4, 2)),
            dma((4, 2, 2)),
            dma((4, 2, 2)),
            dma((2,)),
            dma((2,)),
            dma((groups - 1,)),
            dma((groups - 1,)),
            dma((2,)),
            dma((2,)),
            dma((2, groups - 1)),
            dma((2, groups - 1)),
        ],
        compiler_params=pltpu.CompilerParams(
            collective_id=0, has_side_effects=True, vmem_limit_bytes=60000 * 1024
        ),
        name="tomography",
    )(
        kappa,
        mua,
        prior_forward_fields,
        prior_adjoint_fields,
        source_position,
        detector_voxel,
        detector_voxel.reshape(1, detectors),
        measured_source.reshape(blocks),
        measured_detector.reshape(blocks),
        measured_data.reshape(blocks),
        measured_weight.reshape(blocks),
    )


def solution(mesh):
    in_specs = (
        P("vox", None, None),
        P("vox", None, None),
        P("src", "vox", None, None),
        P("src", "vox", None, None),
        P(),
        P("vox"),
        P(("src", "vox")),
        P(("src", "vox")),
        P(("src", "vox")),
        P(("src", "vox")),
    )
    out_specs = (P("vox", "src", None), P("vox", "src", None))
    return jax.shard_map(body, mesh=mesh, in_specs=in_specs, out_specs=out_specs, check_vma=False)
```

profile of v0, /device:TPU:6, one launch (start us, length us, event | category | flops | bytes accessed | tf_op | source)
XLA Modules:
  0.0 73.4 jit_solution(2570913556303756715)
XLA Ops:
  0.6 70.6 %tomography.1 = (f32[8,8,256]{2,1,0:T(8,128)}, f32[8,8,256]{2,1,0:T(8,128)}) custom-call(f32[8,64,256]{2,1,0:T(8,128)} %kappa.1, f32[8,64,256]{2,1,0:T(8,128)} %mua.1, f32[2,8,64,256]{3,2,1,0:T(8,128)} %prior_fwd.1, f32[2,8,64,256]{3,2,1,0:T(8,128)} %prior_adj.1, s32[16]{0:T(128)} %position.1, s32[128]{0:T(128)} %det_scalar.1, s32[1,128]{1,0:T(1,128)} %bitcast.9, ...), custom_call_target="tpu_custom_call" | custom-call | tf_op jit(solution)/shard_map/tomography/pallas_call | solution.py:571
  71.2 0.0 copy-start
  71.2 1.5 %copy.14 = f32[8,8,256]{2,1,0:T(8,128)} copy(f32[8,8,256]{2,1,0:T(8,128)} %get-tuple-element.4) | data formatting | bytes 131072
  72.7 0.0 copy-done
  72.7 0.6 copy.15
Async XLA Ops:
  71.2 1.5 %copy-start = (f32[8,8,256]{2,1,0:T(8,128)S(1)}, f32[8,8,256]{2,1,0:T(8,128)}, u32[]{:S(2)}) copy-start(f32[8,8,256]{2,1,0:T(8,128)} %get-tuple-element.5) | copy-start | bytes 196612
where the time goes:
time: 73.6 us; the launch traced here: 73.4 us
  Pallas kernels  70.6 us (96%)
  local copies, waits for them, and re-layouts  2.14 us (3%)
    pallas_call x1, Pallas kernels, body(): pl.pallas_call(functools.partial(kernel, groups, slabs), out_shape=(jax.S...  70.6 us
    unnamed x4, local copies, waits for them, and re-layouts  2.14 us

commit v1 on v0

--- a/solution.py
+++ b/solution.py
@@ -8,6 +8,7 @@
 from jax.sharding import PartitionSpec as P
 
 SWEEPS = 6
+SHARE = 4
 LOW = SWEEPS
 HIGH = SWEEPS + 1
 source_gain = 10.0
@@ -98,6 +99,8 @@
     local_sem,
     halo_send,
     halo_recv,
+    relay_send,
+    relay_recv,
     det_send,
     det_recv,
     agg_send,
@@ -163,8 +166,15 @@
         barrier, groups - 1 + jnp.where(has_low, 1, 0) + jnp.where(has_high, 1, 0)
     )
 
-    def halo(array, direction, h):
+    member = lax.rem(src, SHARE)
+    share_rows = 64 // SHARE
+
+    def part_of(who):
+        return pl.ds(pl.multiple_of(share_rows * who, 8), share_rows)
+
+    def halo(array, direction, h, far):
         lanes = pl.ds(128 * h, 128)
+        rows = part_of(member) if far and array < 2 else pl.ds(0, 64)
         if direction == 0:
             count = LOW - 1 if array == 1 else LOW
             start, target = depth - count, LOW - count
@@ -172,8 +182,8 @@
             count = HIGH - 1 if array == 1 else HIGH
             start, target = 0, LOW + depth
         if array < 2:
-            source = (kappa, mua)[array].at[pl.ds(start, count), :, lanes]
-            place = (kap, mu)[array].at[pl.ds(target, count), h]
+            source = (kappa, mua)[array].at[pl.ds(start, count), rows, lanes]
+            place = (kap, mu)[array].at[pl.ds(target, count), h, rows]
         else:
             source = (prior_fwd, prior_adj)[array - 2].at[:, pl.ds(start, count), :, lanes]
             place = (fwd_in, adj_in)[array - 2].at[:, pl.ds(target, count), h]
@@ -186,7 +196,10 @@
             device_id_type=MESH,
         )
 
-    halos = [[[halo(a, d, h) for h in range(2)] for d in range(2)] for a in range(4)]
+    near_halos, far_halos = [
+        [[[halo(a, d, h, far) for h in range(2)] for d in range(2)] for a in range(4)]
+        for far in (False, True)
+    ]
     det_copy = [
         pltpu.make_async_remote_copy(
             src_ref=det_row,
@@ -206,9 +219,46 @@
         @pl.when(sends_to[d])
         def _():
             det_copy[d].start()
-            for a in range(4):
-                for h in range(2):
-                    halos[a][d][h].start()
+
+        for far in (False, True):
+
+            @pl.when(jnp.logical_and(sends_to[d], core == (1 - d if far else d)))
+            def _():
+                for a in range(4):
+                    for h in range(2):
+                        (near_halos, far_halos)[far][a][d][h].start()
+
+    def relay(array, direction, h, step):
+        if direction == 0:
+            count = LOW - 1 if array == 1 else LOW
+            target = LOW - count
+        else:
+            count = HIGH - 1 if array == 1 else HIGH
+            target = LOW + depth
+        place = (kap, mu)[array].at[pl.ds(target, count), h, part_of(member)]
+        return pltpu.make_async_remote_copy(
+            src_ref=place,
+            dst_ref=place,
+            send_sem=relay_send.at[array, h, step - 1],
+            recv_sem=relay_recv.at[array, h, step - 1],
+            device_id={"src": src - member + lax.rem(member + step, SHARE)},
+            device_id_type=MESH,
+        )
+
+    def relays(direction):
+        return [
+            relay(a, direction, h, step)
+            for a in range(2)
+            for h in range(2)
+            for step in range(1, SHARE)
+        ]
+
+    def far_side(action):
+        for d in range(2):
+
+            @pl.when(jnp.logical_and(core == d, gets_from[d]))
+            def _():
+                action(d)
 
     for d in range(2):
 
@@ -334,8 +384,8 @@
     def late(k):
         return pick(k - LOW, depth - k) + LOW, pick(LOW, LOW + 1)
 
-    def solve(fields, part):
-        for k in range(1, SWEEPS + 1):
+    def solve(fields, part, first=1, last=SWEEPS):
+        for k in range(first, last + 1):
             low, count = part(k)
             sweep(fields[(k - 1) % 2], fields[k % 2], low, count)
 
@@ -348,7 +398,7 @@
             def _():
                 for a in arrays:
                     for h in range(2):
-                        halos[a][d][h].wait_recv()
+                        (far_halos, near_halos)[near][a][d][h].wait_recv()
 
     for which in range(4):
         for h in range(2):
@@ -361,7 +411,17 @@
     coefficients(near_low, near_count)
     await_halo((2,), True)
     take_in(fwd_in, field, pick(0, -LOW) + LOW, pick(depth + HIGH, depth + LOW))
-    solve((field, other), early)
+    solve((field, other), early, 1, 2)
+
+    def pass_on(d):
+        for a in range(2):
+            for h in range(2):
+                far_halos[a][d][h].wait_recv()
+        for copy in relays(d):
+            copy.start()
+
+    far_side(pass_on)
+    solve((field, other), early, 3, SWEEPS)
     await_halo((3,), True)
     take_in(adj_in, adjf, pick(0, -LOW) + LOW, pick(depth + HIGH, depth + LOW))
 
@@ -384,7 +444,11 @@
         lane = lax.broadcasted_iota(jnp.int32, (detectors, 256), 1).astype(F32)
         zhot[n] = jnp.where(lane == z_col[:, :1], 1.0, 0.0)
 
-    await_halo((0, 1), False)
+    def shared(d):
+        for copy in relays(d):
+            copy.wait_recv()
+
+    far_side(shared)
     coefficients(far_low, far_count)
     await_halo((2,), False)
     take_in(fwd_in, field, pick(-LOW, depth) + LOW, pick(LOW, HIGH))
@@ -393,14 +457,16 @@
     def gather(d, carry):
         spot = det_scalar[d] - vox * (depth * 64 * 256)
         spot = jnp.clip(spot, 0, depth * 64 * 256 - 1)
-        p = spot // (64 * 256)
-        y = spot // 256 % 64
+        p = lax.shift_right_logical(spot, 14)
+        row = lax.shift_right_logical(spot, 8)
+        slot = lax.bitwise_and(row, 7)
+        sublane = lax.bitwise_and(lax.shift_right_logical(row, 3), 7)
         for s in range(2):
             for h in range(2):
-                picked[s, h, pl.ds(d, 1), :] = field[p + LOW, s, h, y % 8, pl.ds(y // 8, 1), :]
+                picked[s, h, pl.ds(d, 1), :] = field[p + LOW, s, h, slot, pl.ds(sublane, 1), :]
         return carry
 
-    lax.fori_loop(0, detectors, gather, 0)
+    lax.fori_loop(0, detectors, gather, 0, unroll=4)
     for copy in agg_copy:
         copy.wait()
     sums = agg_in[0]
@@ -482,10 +548,13 @@
     await_values(False)
     await_halo((3,), False)
     take_in(adj_in, adjf, pick(-LOW, depth) + LOW, pick(LOW, HIGH))
-    solve((adjf, other), late)
+
+    def stage(j):
+        if j == 0:
+            return lambda k: (pick(k, depth - k) + LOW, pick(0, 1))
+        return lambda k: (pick(k - 2 * j, depth - 1 - k + 2 * j) + LOW, 2)
 
     tile = 64 // groups
-    half_depth = depth // 2
 
     def gradient(i, carry):
         p = i + LOW
@@ -508,9 +577,11 @@
         return carry
 
     grad_copy = []
-    for part in range(2):
-        lax.fori_loop(part * half_depth, (part + 1) * half_depth, gradient, 0)
-        planes = pl.ds(part * half_depth, half_depth)
+    for part in range(depth // 2):
+        solve((adjf, other), stage(part))
+        first = pick(depth - 2 - 2 * part, 2 * part)
+        lax.fori_loop(first, first + 2, gradient, 0)
+        planes = pl.ds(first, 2)
         for step, peer in enumerate(peers):
             copy = pltpu.make_async_remote_copy(
                 src_ref=grad.at[:, planes, :, pl.ds(pl.multiple_of(tile * peer, 8), tile)],
@@ -529,9 +600,20 @@
         def _():
             det_copy[d].wait_send()
             val_copy[d].wait_send()
-            for a in range(4):
-                for h in range(2):
-                    halos[a][d][h].wait_send()
+
+        for far in (False, True):
+
+            @pl.when(jnp.logical_and(sends_to[d], core == (1 - d if far else d)))
+            def _():
+                for a in range(4):
+                    for h in range(2):
+                        (near_halos, far_halos)[far][a][d][h].wait_send()
+
+    def relays_left(d):
+        for copy in relays(d):
+            copy.wait_send()
+
+    far_side(relays_left)
 
     for copy in grad_copy:
         copy.wait()
@@ -595,14 +677,16 @@
             dma((4, 2)),
             dma((4, 2, 2)),
             dma((4, 2, 2)),
+            dma((2, 2, SHARE - 1)),
+            dma((2, 2, SHARE - 1)),
             dma((2,)),
             dma((2,)),
             dma((groups - 1,)),
             dma((groups - 1,)),
             dma((2,)),
             dma((2,)),
-            dma((2, groups - 1)),
-            dma((2, groups - 1)),
+            dma((depth // 2, groups - 1)),
+            dma((depth // 2, groups - 1)),
         ],
         compiler_params=pltpu.CompilerParams(
             collective_id=0, has_side_effects=True, vmem_limit_bytes=60000 * 1024

time: 73.6 us -> 77 us (1.046)
  Pallas kernels: 70.6 us -> 74 us
    pallas_call x1, Pallas kernels: 70.6 us -> 74 us  [body(): pl.pallas_call(functools.partial(kernel, groups, slabs), out_shape=(jax.S...]
where the time goes in v1:
time: 77 us; the launch traced here: 76.8 us
  Pallas kernels  74 us (96%)
  local copies, waits for them, and re-layouts  2.14 us (3%)
    pallas_call x1, Pallas kernels, body(): pl.pallas_call(functools.partial(kernel, groups, slabs), out_shape=(jax.S...  74 us
    unnamed x4, local copies, waits for them, and re-layouts  2.14 us

profile of v1, /device:TPU:6, one launch (start us, length us, event | category | flops | bytes accessed | tf_op | source)
XLA Modules:
  0.0 76.8 jit_solution(14812960135122832455)
XLA Ops:
  0.6 74.0 %tomography.1 = (f32[8,8,256]{2,1,0:T(8,128)}, f32[8,8,256]{2,1,0:T(8,128)}) custom-call(f32[8,64,256]{2,1,0:T(8,128)} %kappa.1, f32[8,64,256]{2,1,0:T(8,128)} %mua.1, f32[2,8,64,256]{3,2,1,0:T(8,128)} %prior_fwd.1, f32[2,8,64,256]{3,2,1,0:T(8,128)} %prior_adj.1, s32[16]{0:T(128)} %position.1, s32[128]{0:T(128)} %det_scalar.1, s32[1,128]{1,0:T(1,128)} %bitcast.9, ...), custom_call_target="tpu_custom_call" | custom-call | tf_op jit(solution)/shard_map/tomography/pallas_call | solution.py:653
  74.6 0.0 copy-start
  74.7 1.5 %copy.14 = f32[8,8,256]{2,1,0:T(8,128)} copy(f32[8,8,256]{2,1,0:T(8,128)} %get-tuple-element.4) | data formatting | bytes 131072
  76.2 0.0 copy-done
  76.2 0.6 copy.15
Async XLA Ops:
  74.6 1.5 %copy-start = (f32[8,8,256]{2,1,0:T(8,128)S(1)}, f32[8,8,256]{2,1,0:T(8,128)}, u32[]{:S(2)}) copy-start(f32[8,8,256]{2,1,0:T(8,128)} %get-tuple-element.5) | copy-start | bytes 196612

commit v2 on v0

--- a/solution.py
+++ b/solution.py
@@ -393,14 +393,16 @@
     def gather(d, carry):
         spot = det_scalar[d] - vox * (depth * 64 * 256)
         spot = jnp.clip(spot, 0, depth * 64 * 256 - 1)
-        p = spot // (64 * 256)
-        y = spot // 256 % 64
+        p = lax.shift_right_logical(spot, 14)
+        row = lax.shift_right_logical(spot, 8)
+        slot = lax.bitwise_and(row, 7)
+        sublane = lax.bitwise_and(lax.shift_right_logical(row, 3), 7)
         for s in range(2):
             for h in range(2):
-                picked[s, h, pl.ds(d, 1), :] = field[p + LOW, s, h, y % 8, pl.ds(y // 8, 1), :]
+                picked[s, h, pl.ds(d, 1), :] = field[p + LOW, s, h, slot, pl.ds(sublane, 1), :]
         return carry
 
-    lax.fori_loop(0, detectors, gather, 0)
+    lax.fori_loop(0, detectors, gather, 0, unroll=4)
     for copy in agg_copy:
         copy.wait()
     sums = agg_in[0]
@@ -482,10 +484,13 @@
     await_values(False)
     await_halo((3,), False)
     take_in(adj_in, adjf, pick(-LOW, depth) + LOW, pick(LOW, HIGH))
-    solve((adjf, other), late)
+
+    def stage(j):
+        if j == 0:
+            return lambda k: (pick(k, depth - k) + LOW, pick(0, 1))
+        return lambda k: (pick(k - 2 * j, depth - 1 - k + 2 * j) + LOW, 2)
 
     tile = 64 // groups
-    half_depth = depth // 2
 
     def gradient(i, carry):
         p = i + LOW
@@ -508,9 +513,11 @@
         return carry
 
     grad_copy = []
-    for part in range(2):
-        lax.fori_loop(part * half_depth, (part + 1) * half_depth, gradient, 0)
-        planes = pl.ds(part * half_depth, half_depth)
+    for part in range(depth // 2):
+        solve((adjf, other), stage(part))
+        first = pick(depth - 2 - 2 * part, 2 * part)
+        lax.fori_loop(first, first + 2, gradient, 0)
+        planes = pl.ds(first, 2)
         for step, peer in enumerate(peers):
             copy = pltpu.make_async_remote_copy(
                 src_ref=grad.at[:, planes, :, pl.ds(pl.multiple_of(tile * peer, 8), tile)],
@@ -601,8 +608,8 @@
             dma((groups - 1,)),
             dma((2,)),
             dma((2,)),
-            dma((2, groups - 1)),
-            dma((2, groups - 1)),
+            dma((depth // 2, groups - 1)),
+            dma((depth // 2, groups - 1)),
         ],
         compiler_params=pltpu.CompilerParams(
             collective_id=0, has_side_effects=True, vmem_limit_bytes=60000 * 1024

time: 73.6 us -> 68.8 us (0.935)
  Pallas kernels: 70.6 us -> 65.8 us
    pallas_call x1, Pallas kernels: 70.6 us -> 65.8 us  [body(): pl.pallas_call(functools.partial(kernel, groups, slabs), out_shape=(jax.S...]
where the time goes in v2:
time: 68.8 us; the launch traced here: 68.6 us
  Pallas kernels  65.8 us (96%)
  local copies, waits for them, and re-layouts  2.14 us (3%)
    pallas_call x1, Pallas kernels, body(): pl.pallas_call(functools.partial(kernel, groups, slabs), out_shape=(jax.S...  65.8 us
    unnamed x4, local copies, waits for them, and re-layouts  2.14 us

profile of v2, /device:TPU:6, one launch (start us, length us, event | category | flops | bytes accessed | tf_op | source)
XLA Modules:
  0.0 68.6 jit_solution(14572566200494277604)
XLA Ops:
  0.6 65.8 %tomography.1 = (f32[8,8,256]{2,1,0:T(8,128)}, f32[8,8,256]{2,1,0:T(8,128)}) custom-call(f32[8,64,256]{2,1,0:T(8,128)} %kappa.1, f32[8,64,256]{2,1,0:T(8,128)} %mua.1, f32[2,8,64,256]{3,2,1,0:T(8,128)} %prior_fwd.1, f32[2,8,64,256]{3,2,1,0:T(8,128)} %prior_adj.1, s32[16]{0:T(128)} %position.1, s32[128]{0:T(128)} %det_scalar.1, s32[1,128]{1,0:T(1,128)} %bitcast.9, ...), custom_call_target="tpu_custom_call" | custom-call | tf_op jit(solution)/shard_map/tomography/pallas_call | solution.py:578
  66.4 0.0 copy-start
  66.4 1.5 %copy.14 = f32[8,8,256]{2,1,0:T(8,128)} copy(f32[8,8,256]{2,1,0:T(8,128)} %get-tuple-element.4) | data formatting | bytes 131072
  67.9 0.0 copy-done
  68.0 0.6 copy.15
Async XLA Ops:
  66.4 1.5 %copy-start = (f32[8,8,256]{2,1,0:T(8,128)S(1)}, f32[8,8,256]{2,1,0:T(8,128)}, u32[]{:S(2)}) copy-start(f32[8,8,256]{2,1,0:T(8,128)} %get-tuple-element.5) | copy-start | bytes 196612

commit v3 on v2

--- a/solution.py
+++ b/solution.py
@@ -75,8 +75,7 @@
     row_detector,
     row_data,
     row_weight,
-    out_mua,
-    out_kappa,
+    out,
     kap,
     mu,
     fwd_in,
@@ -117,7 +116,11 @@
     has_high = vox < slabs - 1
     below = {"vox": jnp.maximum(vox - 1, 0)}
     above = {"vox": jnp.minimum(vox + 1, slabs - 1)}
-    peers = [lax.rem(src + step, groups) for step in range(1, groups)]
+    row, side = src // 2, lax.rem(src, 2)
+    peers = [
+        lax.rem(row + down, groups // 2) * 2 + lax.rem(side + across, 2)
+        for down, across in ((2, 1), (1, 0), (3, 0), (2, 0), (1, 1), (3, 1), (0, 1))
+    ]
 
     barrier = pltpu.get_barrier_semaphore()
 
@@ -543,12 +546,12 @@
     for copy in grad_copy:
         copy.wait()
     mine = pl.ds(pl.multiple_of(tile * src, 8), tile)
-    for q, out in ((0, out_mua), (1, out_kappa)):
+    for q in range(2):
         for h in range(2):
             value = grad[q, :, h, mine, :]
             for step in range(groups - 1):
                 value = value + grad_in[step, q, :, h]
-            out[:, :, 128 * h : 128 * h + 128] = value
+            out[q, :, :, 128 * h : 128 * h + 128] = value
 
 
 def body(
@@ -575,11 +578,11 @@
     tile = width // groups
     dma = pltpu.SemaphoreType.DMA
     slab_field = pltpu.VMEM((total, 2, 2, 8, 8, 128), F32)
-    return pl.pallas_call(
+    both = pl.pallas_call(
         functools.partial(kernel, groups, slabs),
-        out_shape=(jax.ShapeDtypeStruct((depth, tile, 256), F32),) * 2,
+        out_shape=jax.ShapeDtypeStruct((2, depth, tile, 256), F32),
         in_specs=[hbm] * 4 + [smem] * 2 + [vmem] * 5,
-        out_specs=(vmem, vmem),
+        out_specs=vmem,
         scratch_shapes=[
             pltpu.VMEM((total, 2, 64, 128), F32),
             pltpu.VMEM((total, 2, 64, 128), F32),
@@ -628,6 +631,7 @@
         measured_data.reshape(blocks),
         measured_weight.reshape(blocks),
     )
+    return both[0], both[1]
 
 
 def solution(mesh):

time: 68.8 us -> 67.7 us (0.984)
    unnamed x4 -> x0, local copies, waits for them, and re-layouts: 2.14 us -> none
    squeeze x0 -> x1, local copies, waits for them, and re-layouts: none -> 1.53 us  [body(): return (both[0], both[1])]
where the time goes in v3:
time: 67.7 us; the launch traced here: 67.6 us
  Pallas kernels  65.4 us (97%)
  local copies, waits for them, and re-layouts  1.53 us (2%)
    pallas_call x1, Pallas kernels, body(): pl.pallas_call(functools.partial(kernel, groups, slabs), out_shape=jax.Sh...  65.4 us
    squeeze x1, local copies, waits for them, and re-layouts, body(): return (both[0], both[1])  1.53 us

profile of v3, /device:TPU:6, one launch (start us, length us, event | category | flops | bytes accessed | tf_op | source)
XLA Modules:
  0.0 67.6 jit_solution(5652220587750909042)
XLA Ops:
  0.6 65.4 %tomography.1 = f32[2,8,8,256]{3,2,1,0:T(8,128)} custom-call(f32[8,64,256]{2,1,0:T(8,128)} %kappa.1, f32[8,64,256]{2,1,0:T(8,128)} %mua.1, f32[2,8,64,256]{3,2,1,0:T(8,128)} %prior_fwd.1, f32[2,8,64,256]{3,2,1,0:T(8,128)} %prior_adj.1, s32[16]{0:T(128)} %position.1, s32[128]{0:T(128)} %det_scalar.1, s32[1,128]{1,0:T(1,128)} %bitcast.13, s32[8,128]{1,0:T(8,128)} %bitcast.9, ...), custom_call_target="tpu_custom_call" | custom-call | tf_op jit(solution)/shard_map/tomography/pallas_call | solution.py:581
  66.0 1.5 %slice_bitcast_fusion = (f32[8,8,256]{2,1,0:T(8,128)}, f32[8,8,256]{2,1,0:T(8,128)}) fusion(f32[2,8,8,256]{3,2,1,0:T(8,128)} %tomography.1), kind=kLoop, calls=%fused_computation | loop fusion | bytes 262144 | tf_op jit(solution)/shard_map/squeeze | solution.py:634
